TPU v7x, 32 devices: a whole 2x2x4 slice. The times are simulated.
32 devices in a mesh: row: 16 (over z, y, core), col: 2 (over x).
Axes of the slice: x: 2, y: 2, z: 4, core: 2. Of those that a mesh axis runs over, the one named last changes fastest.
Arguments:
- start_block: float32 [4096, 256], P(('row', 'col')), may hold values from -6 to 6
- tiles: bfloat16 [16, 2, 14, 128, 128], P('row', 'col'), may hold values from -0.125 to 0.125
- tile_rows: int32 [16, 2, 14], P('row', 'col'), may hold values from -1 to 31, as said below
- tile_cols: int32 [16, 2, 14], P('row', 'col'), may hold values from -1 to 31, as said below
- bounds: float32 [3], replicated, may hold values from -2.6 to 2.6, as said below
Outputs:
- filtered: float32 [4096, 256], P(('row', 'col'))
Inputs may be any that keep to these rules, and one draw needn't show every extreme that they name: Vector rows form blocks of 128 rows, one block a device, in row+col order. On the device at grid row r and grid column c, a live slot names a block row held by one of the devices (r, any column) and a block column held by one of the devices (any row, c). Live slots come first; each device has 1 to 14 live slots, and one device has exactly 14 in every draw. No block position is named twice, and the mirror of a named position is never named unless it lies on the diagonal. tile_rows and tile_cols are -1 together. `tile_cols`: same slots as tile_rows. bounds[0] < bounds[1] < bounds[2].
All inputs are finite; a program needn't handle non-finite values.
Results may differ from a plain program's by a relative error of at most 0.0042.
Values may be sent and summed in bfloat16 or wider, within the bound.
A program may use at most 64 MiB of HBM per device.

v0:
```python
import jax
import jax.numpy as jnp
from jax import lax
from jax.sharding import PartitionSpec as P

DEGREE = 4


def local(start_block, tiles, tile_rows, tile_cols, bounds):
    rows_dev, vec_width = start_block.shape
    tile_size = tiles.shape[-1]
    blocks = rows_dev // tile_size
    row_count = lax.axis_size("row")
    col_count = lax.axis_size("col")
    near_count = col_count * blocks
    far_count = row_count * blocks
    row_index = lax.axis_index("row")
    col_index = lax.axis_index("col")
    slots = tiles.shape[2]
    tile_mats = tiles.reshape(slots, tile_size, tile_size)
    glob_rows = tile_rows.reshape(slots)
    glob_cols = tile_cols.reshape(slots)
    is_live = glob_rows >= 0
    local_rows = jnp.where(is_live, glob_rows - row_index * near_count, -1)
    local_cols = jnp.where(
        is_live, glob_cols // blocks // col_count * blocks + glob_cols % blocks, -1
    )
    slot_place = jnp.where(is_live, local_rows * far_count + local_cols, near_count * far_count)
    owned = jnp.zeros((near_count * far_count, tile_size, tile_size), jnp.bfloat16)
    owned = owned.at[slot_place].add(tile_mats, mode="drop")
    owned = owned.reshape(col_count, blocks, row_count, blocks, tile_size, tile_size)
    received = lax.all_to_all(
        lax.all_to_all(owned, "row", split_axis=2, concat_axis=2, tiled=True),
        "col",
        split_axis=0,
        concat_axis=0,
        tiled=True,
    )
    mirror = jnp.transpose(received, (0, 3, 2, 1, 5, 4))
    grid_shape = (col_count, blocks, row_count, blocks)
    col_grid = lax.broadcasted_iota(jnp.int32, grid_shape, 0)
    first_sub = lax.broadcasted_iota(jnp.int32, grid_shape, 1)
    row_grid = lax.broadcasted_iota(jnp.int32, grid_shape, 2)
    second_sub = lax.broadcasted_iota(jnp.int32, grid_shape, 3)
    on_diagonal = (col_grid == col_index) & (row_grid == row_index) & (first_sub == second_sub)
    zero_tile = jnp.zeros((), jnp.bfloat16)
    window = (jnp.where(on_diagonal[..., None, None], zero_tile, owned) + mirror).reshape(
        near_count, far_count, tile_size, tile_size
    )
    owned_here = lax.dynamic_index_in_dim(owned, col_index, 0, keepdims=False)
    owned_here = lax.dynamic_index_in_dim(owned_here, row_index, 1, keepdims=False)
    block_ids = jnp.arange(blocks)
    diagonal_tiles = owned_here[block_ids, block_ids]

    def apply_matrix(vectors):
        low_vectors = vectors.astype(jnp.bfloat16)
        far_vectors = lax.all_gather(low_vectors, "row", axis=0, tiled=True).reshape(
            far_count, tile_size, vec_width
        )
        near_partial = jnp.einsum(
            "apxy,pyk->axk", window, far_vectors, preferred_element_type=jnp.float32
        )
        own_vectors = lax.dynamic_slice_in_dim(far_vectors, row_index * blocks, blocks, 0)
        diagonal_part = jnp.einsum(
            "uxy,uyk->uxk", diagonal_tiles, own_vectors, preferred_element_type=jnp.float32
        )
        current_rows = lax.dynamic_slice_in_dim(near_partial, col_index * blocks, blocks, 0)
        near_partial = lax.dynamic_update_slice_in_dim(
            near_partial, current_rows + diagonal_part, col_index * blocks, 0
        )
        combined = lax.psum_scatter(
            near_partial.reshape(near_count * tile_size, vec_width),
            "col",
            scatter_dimension=0,
            tiled=True,
        )
        return combined

    half_width = (bounds[2] - bounds[1]) * 0.5
    center = (bounds[2] + bounds[1]) * 0.5
    sigma_one = half_width / (bounds[0] - center)
    previous = start_block
    current = (apply_matrix(start_block) - center * start_block) * (sigma_one / half_width)
    sigma = sigma_one
    for turn_index in range(DEGREE - 1):
        sigma_next = 1.0 / (2.0 / sigma_one - sigma)
        product = apply_matrix(current)
        following = (product - center * current) * (
            2.0 * sigma_next / half_width
        ) - sigma * sigma_next * previous
        previous = current
        current = following
        sigma = sigma_next
    return current


def solution(mesh):
    placed = (
        P(("row", "col"), None),
        P("row", "col", None, None, None),
        P("row", "col", None),
        P("row", "col", None),
        P(),
    )
    return jax.shard_map(
        local, mesh=mesh, in_specs=placed, out_specs=P(("row", "col"), None), check_vma=False
    )
```

profile of v0, /device:TPU:0, one launch (start us, length us, event | category | flops | bytes accessed | tf_op | source)
XLA Modules:
  0.0 251.6 jit_solution(16781734857981256183)
XLA Ops:
  8.2 2.1 scatter_fusion
  10.3 1.3 copy.9
  11.6 7.5 %all-to-all-start = ((bf16[2,1,16,1,128,128]{4,5,0,1,3,2:T(8,128)(2,1)}), bf16[2,1,16,1,128,128]{4,5,0,1,3,2:T(8,128)(2,1)S(1)}, u32[]{:S(2)}, u32[]{:S(2)}) async-start(bf16[2,1,16,1,128,128]{4,5,0,1,3,2:T(8,128)(2,1)} %copy.9), calls=%async_computation | async-start | bytes 2097152 | tf_op jit(solution)/shard_map/all_to_all | solution.py:33
  19.9 23.3 %all-to-all-done = bf16[2,1,16,1,128,128]{4,5,0,1,3,2:T(8,128)(2,1)S(1)} async-done(((bf16[2,1,16,1,128,128]{4,5,0,1,3,2:T(8,128)(2,1)}), bf16[2,1,16,1,128,128]{4,5,0,1,3,2:T(8,128)(2,1)S(1)}, u32[]{:S(2)}, u32[]{:S(2)}) %all-to-all-start) | async-done | bytes 1048608 | tf_op jit(solution)/shard_map/all_to_all | solution.py:33
  43.2 1.1 copy.10
  44.3 3.6 %all-to-all-start.1 = ((bf16[2,1,16,1,128,128]{4,5,2,1,3,0:T(8,128)(2,1)}), bf16[2,1,16,1,128,128]{4,5,2,1,3,0:T(8,128)(2,1)S(1)}, u32[]{:S(2)}, u32[]{:S(2)}) async-start(bf16[2,1,16,1,128,128]{4,5,2,1,3,0:T(8,128)(2,1)} %copy.10), calls=%async_computation.1 | async-start | bytes 2097152 | tf_op jit(solution)/shard_map/all_to_all | solution.py:32
  48.0 14.3 %all-to-all-done.1 = bf16[2,1,16,1,128,128]{4,5,2,1,3,0:T(8,128)(2,1)S(1)} async-done(((bf16[2,1,16,1,128,128]{4,5,2,1,3,0:T(8,128)(2,1)}), bf16[2,1,16,1,128,128]{4,5,2,1,3,0:T(8,128)(2,1)S(1)}, u32[]{:S(2)}, u32[]{:S(2)}) %all-to-all-start.1) | async-done | bytes 1048608 | tf_op jit(solution)/shard_map/all_to_all | solution.py:32
  62.5 3.5 %all-gather.5.cloned.1.call-done = bf16[2048,256]{1,0:T(8,128)(2,1)} async-done(((bf16[128,256]{1,0:T(8,128)(2,1)}), bf16[2048,256]{1,0:T(8,128)(2,1)}) %all-gather.5.cloned.1.call-update) | async-done | bytes 1048592 | tf_op jit(solution)/shard_map/all_gather | solution.py:57
  66.0 1.7 convolution_bitcast_fusion.3
  67.6 1.0 fusion.1
  73.3 7.0 %reduce-scatter.5.cloned.1.call-done = f32[128,256]{1,0:T(8,128)} async-done(((f32[256,256]{1,0:T(8,128)}), f32[128,256]{1,0:T(8,128)}) %reduce-scatter.5.cloned.1.call-update) | async-done | bytes 131088 | tf_op jit(solution)/shard_map/reduce_scatter | solution.py:71
  80.2 1.6 fusion.37
  81.9 38.5 %all-gather.7.cloned.1.call-done = bf16[2048,256]{1,0:T(8,128)(2,1)} async-done(((bf16[128,256]{1,0:T(8,128)(2,1)}), bf16[2048,256]{1,0:T(8,128)(2,1)}) %all-gather.7.cloned.1.call-update) | async-done | bytes 1048592 | tf_op jit(solution)/shard_map/all_gather | solution.py:57
  120.3 1.7 convolution_bitcast_fusion.2
  123.9 10.6 %reduce-scatter.7.cloned.1.call-done = f32[128,256]{1,0:T(8,128)} async-done(((f32[256,256]{1,0:T(8,128)}), f32[128,256]{1,0:T(8,128)}) %reduce-scatter.7.cloned.1.call-update) | async-done | bytes 131088 | tf_op jit(solution)/shard_map/reduce_scatter | solution.py:71
  134.6 1.6 fusion.36
  136.2 38.3 %all-gather.9.cloned.1.call-done = bf16[2048,256]{1,0:T(8,128)(2,1)} async-done(((bf16[128,256]{1,0:T(8,128)(2,1)}), bf16[2048,256]{1,0:T(8,128)(2,1)}) %all-gather.9.cloned.1.call-update) | async-done | bytes 1048592 | tf_op jit(solution)/shard_map/all_gather | solution.py:57
  174.5 1.7 convolution_bitcast_fusion.1
  178.0 10.8 %reduce-scatter.9.cloned.1.call-done = f32[128,256]{1,0:T(8,128)} async-done(((f32[256,256]{1,0:T(8,128)}), f32[128,256]{1,0:T(8,128)}) %reduce-scatter.9.cloned.1.call-update) | async-done | bytes 131088 | tf_op jit(solution)/shard_map/reduce_scatter | solution.py:71
  188.8 1.6 fusion.24
  190.4 38.4 %all-gather.11.cloned.1.call-done = bf16[2048,256]{1,0:T(8,128)(2,1)} async-done(((bf16[128,256]{1,0:T(8,128)(2,1)}), bf16[2048,256]{1,0:T(8,128)(2,1)}) %all-gather.11.cloned.1.call-update) | async-done | bytes 1048592 | tf_op jit(solution)/shard_map/all_gather | solution.py:57
  228.8 1.7 convolution_bitcast_fusion
  232.3 10.8 %reduce-scatter.11.cloned.1.call-done = f32[128,256]{1,0:T(8,128)} async-done(((f32[256,256]{1,0:T(8,128)}), f32[128,256]{1,0:T(8,128)}) %reduce-scatter.11.cloned.1.call-update) | async-done | bytes 131088 | tf_op jit(solution)/shard_map/reduce_scatter | solution.py:71
  243.1 1.6 multiply_subtract_fusion
  (47 shorter events, 9.5 us)
Async XLA Ops:
  6.5 0.7 copy-start.8
  6.5 0.7 copy-start.9
  7.2 1.0 copy-start.6
  11.6 7.6 %copy-start.4 = (f32[128,256]{1,0:T(8,128)S(1)}, f32[128,256]{1,0:T(8,128)}, u32[]{:S(2)}) copy-start(f32[128,256]{1,0:T(8,128)} %param.5) | copy-start | bytes 393220
  11.6 31.6 %all-to-all-start = ((bf16[2,1,16,1,128,128]{4,5,0,1,3,2:T(8,128)(2,1)}), bf16[2,1,16,1,128,128]{4,5,0,1,3,2:T(8,128)(2,1)S(1)}, u32[]{:S(2)}, u32[]{:S(2)}) async-start(bf16[2,1,16,1,128,128]{4,5,0,1,3,2:T(8,128)(2,1)} %copy.9), calls=%async_computation | async-start | bytes 2097152 | tf_op jit(solution)/shard_map/all_to_all | solution.py:33
  19.2 46.8 %all-gather.5.cloned.1.call-start = ((), (), s32[]{:S(2)}) async-start(), calls=%async_computation.6 | async-start | bytes 1114112 | tf_op jit(solution)/shard_map/all_gather | solution.py:57
  44.3 18.0 %all-to-all-start.1 = ((bf16[2,1,16,1,128,128]{4,5,2,1,3,0:T(8,128)(2,1)}), bf16[2,1,16,1,128,128]{4,5,2,1,3,0:T(8,128)(2,1)S(1)}, u32[]{:S(2)}, u32[]{:S(2)}) async-start(bf16[2,1,16,1,128,128]{4,5,2,1,3,0:T(8,128)(2,1)} %copy.10), calls=%async_computation.1 | async-start | bytes 2097152 | tf_op jit(solution)/shard_map/all_to_all | solution.py:32
  47.9 32.4 %reduce-scatter.5.cloned.1.call-start = ((), (), s32[]{:S(2)}) async-start(), calls=%async_computation.7 | async-start | bytes 393216 | tf_op jit(solution)/shard_map/reduce_scatter | solution.py:71
  68.6 0.7 copy-start.1
  68.6 0.8 copy-start.7
  69.3 51.0 %all-gather.7.cloned.1.call-start = ((), (), s32[]{:S(2)}) async-start(), calls=%async_computation.8 | async-start | bytes 1114112 | tf_op jit(solution)/shard_map/all_gather | solution.py:57
  81.8 52.8 %reduce-scatter.7.cloned.1.call-start = ((), (), s32[]{:S(2)}) async-start(), calls=%async_computation.9 | async-start | bytes 393216 | tf_op jit(solution)/shard_map/reduce_scatter | solution.py:71
  123.0 0.7 copy-start.2
  123.7 50.8 %all-gather.9.cloned.1.call-start = ((), (), s32[]{:S(2)}) async-start(), calls=%async_computation.10 | async-start | bytes 1114112 | tf_op jit(solution)/shard_map/all_gather | solution.py:57
  136.2 52.6 %reduce-scatter.9.cloned.1.call-start = ((), (), s32[]{:S(2)}) async-start(), calls=%async_computation.11 | async-start | bytes 393216 | tf_op jit(solution)/shard_map/reduce_scatter | solution.py:71
  177.2 0.7 copy-start.3
  177.9 50.9 %all-gather.11.cloned.1.call-start = ((), (), s32[]{:S(2)}) async-start(), calls=%async_computation.12 | async-start | bytes 1114112 | tf_op jit(solution)/shard_map/all_gather | solution.py:57
  190.4 52.7 %reduce-scatter.11.cloned.1.call-start = ((), (), s32[]{:S(2)}) async-start(), calls=%async_computation.13 | async-start | bytes 393216 | tf_op jit(solution)/shard_map/reduce_scatter | solution.py:71
  231.5 0.7 copy-start
  231.5 11.6 %copy-start.5 = (f32[128,256]{1,0:T(8,128)S(1)}, f32[128,256]{1,0:T(8,128)}, u32[]{:S(2)}) copy-start(f32[128,256]{1,0:T(8,128)} %reduce-scatter.9.cloned.1.call-done) | copy-start | bytes 393220
Sparse Core Ops, SparseCore 0:
  22.2 43.7 all-gather.4
  69.5 10.7 reduce-scatter.4
  82.4 37.8 all-gather.6
  123.8 10.6 reduce-scatter.6
  136.6 37.8 all-gather.8
  178.0 10.7 reduce-scatter.8
  191.0 37.8 all-gather.10
  232.4 10.6 reduce-scatter.10
where the time goes:
time: 252 us
  waiting for transfers between devices  195 us (77%)
  between operations  17.2 us (7%)
  starting transfers between devices  11.5 us (5%)
  matrix products  10.6 us (4%)
  other arithmetic  9.26 us (4%)
  local copies, waits for them, and re-layouts  7.51 us (3%)
    all_gather x4, waiting for transfers between devices, apply_matrix(): lax.all_gather(low_vectors, 'row', axis=0, tiled=True)  119 us
    reduce_scatter x4, waiting for transfers between devices, apply_matrix(): lax.psum_scatter(near_partial.reshape(near_count * tile_size, vec_width),...  39.2 us
    all_to_all x1, waiting for transfers between devices, local(): lax.all_to_all(owned, 'row', split_axis=2, concat_axis=2, tiled=True)  23.3 us
    all_to_all x1, waiting for transfers between devices, local(): lax.all_to_all(lax.all_to_all(owned, 'row', split_axis=2, concat_axis=2,...  14.3 us
    all_to_all x1, starting transfers between devices, local(): lax.all_to_all(owned, 'row', split_axis=2, concat_axis=2, tiled=True)  7.54 us
    dot_general x4, matrix products, apply_matrix(): jnp.einsum('apxy,pyk->axk', window, far_vectors, preferred_element_type=j...  6.63 us
    convert_element_type x4, other arithmetic, apply_matrix(): low_vectors = vectors.astype(jnp.bfloat16)  5.32 us
  transfers between devices with their start and end apart: 10, of which 10 were waited for; matrix products, arithmetic and copies ran while one was open for 1% of the time, Pallas kernels for 0%

commit v1 on v0

v1 whole, which is shorter than its diff:
```python
import functools

import jax
import jax.numpy as jnp
from jax import lax
from jax.experimental import pallas as pl
from jax.experimental.pallas import tpu as pltpu
from jax.sharding import PartitionSpec as P

DEGREE = 4
CHAINS = 1
MESH = pl.DeviceIdType.MESH


def kernel(
    far, near, slots, tile, width,
    rows_ref, cols_ref, bounds_ref, start_ref, tiles_ref, out_ref,
    placed, owned, mirror, window, diagonal, low, partial, arrived, mine, state,
    tile_send, tile_recv, low_send, low_recv, part_send, part_recv,
):
    chips = far // 2
    tall = far // 4
    count = far * near
    cut = width // CHAINS
    row = lax.axis_index("row")
    col = lax.axis_index("col")
    me = row * near + col
    core = row % 2
    mid = row // 2 % 2
    high = row // 4

    def spot(high_at, mid_at, core_at):
        return core_at * chips + high_at * 2 + mid_at

    def row_of(high_at, mid_at, core_at):
        return (high_at * 2 + mid_at) * 2 + core_at

    own_spot = spot(high, mid, core)

    barrier = pltpu.get_barrier_semaphore()

    def greet(step, carry):
        other = (me + step) % count
        pl.semaphore_signal(
            barrier, inc=1, device_id=(other // near, other % near), device_id_type=MESH
        )
        return carry

    lax.fori_loop(1, count, greet, 0)

    line = (1, cut)
    lowest = jnp.full(line, bounds_ref[0], jnp.float32)
    lower = jnp.full(line, bounds_ref[1], jnp.float32)
    upper = jnp.full(line, bounds_ref[2], jnp.float32)
    half_width = (upper - lower) * 0.5
    center = (upper + lower) * 0.5
    sigma_one = half_width / (lowest - center)

    def columns(chain):
        return slice(chain * cut, (chain + 1) * cut)

    for chain in range(CHAINS):
        low[0, chain, own_spot] = start_ref[:, columns(chain)].astype(jnp.bfloat16)

    for slot in range(slots):
        placed[slot] = tiles_ref[slot]
    placed[slots] = jnp.zeros((tile, tile), jnp.bfloat16)
    places = []
    for slot in range(slots):
        glob_row = rows_ref[slot]
        glob_col = cols_ref[slot]
        place = (glob_col // near) * near + (glob_row - row * near)
        places.append(jnp.where(glob_row >= 0, place, -1))

    def put(position, carry):
        chosen = jnp.int32(slots)
        for slot in range(slots):
            chosen = jnp.where(places[slot] == position, slot, chosen)
        owned[position] = placed[chosen]
        return carry

    lax.fori_loop(0, count, put, 0)
    diagonal[...] = owned[me]
    mirror[me] = diagonal[...]
    owned[me] = jnp.zeros((tile, tile), jnp.bfloat16)

    pl.semaphore_wait(barrier, count - 1)

    def send_low(step, chain, place, target_row):
        pltpu.make_async_remote_copy(
            src_ref=low.at[step, chain, place],
            dst_ref=low.at[step, chain, place],
            send_sem=low_send.at[step, chain],
            recv_sem=low_recv.at[step, chain, place],
            device_id=(target_row, col),
            device_id_type=MESH,
        ).start()

    def await_low(step, chain, place):
        here = low.at[step, chain, place]
        pltpu.make_async_copy(here, here, low_recv.at[step, chain, place]).wait()

    def begin(step, chain):
        for offset in range(1, tall):
            send_low(step, chain, own_spot, row_of((high + offset) % tall, mid, core))
        send_low(step, chain, own_spot, row_of(high, 1 - mid, core))
        send_low(step, chain, own_spot, row_of(high, mid, 1 - core))

    def forward_line(step, chain):
        for offset in range(1, tall):
            place = spot((high + offset) % tall, mid, core)
            await_low(step, chain, place)
            send_low(step, chain, place, row_of(high, 1 - mid, core))
            send_low(step, chain, place, row_of(high, mid, 1 - core))

    def forward_mid(step, chain):
        for offset in range(tall):
            place = spot((high + offset) % tall, 1 - mid, core)
            await_low(step, chain, place)
            send_low(step, chain, place, row_of(high, mid, 1 - core))

    def await_core(step, chain):
        for offset in range(tall):
            for mid_at in range(2):
                await_low(step, chain, spot((high + offset) % tall, mid_at, 1 - core))

    def send_tile(step, carry):
        other = (me + step) % count
        pltpu.make_async_remote_copy(
            src_ref=owned.at[other],
            dst_ref=mirror.at[me],
            send_sem=tile_send,
            recv_sem=tile_recv.at[row],
            device_id=(other // near, other % near),
            device_id_type=MESH,
        ).start()
        return carry

    def build(step, carry):
        source = (row + far - step) % far
        base = source * near
        group = mirror.at[pl.ds(base, near)]
        pltpu.make_async_copy(group, group, tile_recv.at[source]).wait()
        fill(source)
        return carry

    def fill(source):
        lanes = (source % 2) * chips + source // 2
        lanes = pl.ds(pl.multiple_of(lanes * tile, tile), tile)
        for near_at in range(near):
            index = source * near + near_at
            window[near_at * tile : (near_at + 1) * tile, lanes] = (
                owned[index] + mirror[index].T
            )

    def multiply(step, chain, near_at):
        total = jnp.zeros((tile, cut), jnp.float32)
        matrix = window[pl.ds(pl.multiple_of(near_at * tile, tile), tile), :]
        vectors = low[step, chain].reshape(far * tile, cut)
        return total + jnp.dot(matrix, vectors, preferred_element_type=jnp.float32)

    def product(step, chain):
        for offset in range(1, near):
            other = (col + offset) % near
            partial[step, chain, other] = multiply(step, chain, other)
            pltpu.make_async_remote_copy(
                src_ref=partial.at[step, chain, other],
                dst_ref=arrived.at[step, chain, col],
                send_sem=part_send.at[step, chain],
                recv_sem=part_recv.at[step, chain, col],
                device_id=(row, other),
                device_id_type=MESH,
            ).start()
        mine[chain] = multiply(step, chain, col) + jnp.dot(
            diagonal[...], low[step, chain, own_spot], preferred_element_type=jnp.float32
        )

    def finish(step, chain, sigma):
        total = mine[chain]
        for offset in range(1, near):
            other = (col + offset) % near
            here = arrived.at[step, chain, other]
            pltpu.make_async_copy(here, here, part_recv.at[step, chain, other]).wait()
            total = total + arrived[step, chain, other]
        where = columns(chain)
        current = start_ref[:, where] if step == 0 else state[step - 1, :, where]
        if step == 0:
            following = (total - center * current) * (sigma_one / half_width)
            sigma_next = sigma_one
        else:
            before = start_ref[:, where] if step == 1 else state[step - 2, :, where]
            sigma_next = 1.0 / (2.0 / sigma_one - sigma)
            following = (total - center * current) * (
                2.0 * sigma_next / half_width
            ) - (sigma * sigma_next) * before
        if step == DEGREE - 1:
            out_ref[:, where] = following
        else:
            low[step + 1, chain, own_spot] = following.astype(jnp.bfloat16)
            begin(step + 1, chain)
            state[step, :, where] = following
        return sigma_next

    for chain in range(CHAINS):
        begin(0, chain)
    lax.fori_loop(1, count // 2, send_tile, 0)
    for chain in range(CHAINS):
        forward_line(0, chain)
    lax.fori_loop(count // 2, count, send_tile, 0)
    for chain in range(CHAINS):
        forward_mid(0, chain)

    if near > 1:
        group = mirror.at[pl.ds(row * near, near - 1)]
        pltpu.make_async_copy(group, group, tile_recv.at[row]).wait()
    fill(row)
    lax.fori_loop(1, far, build, 0)

    sigma = sigma_one
    for step in range(DEGREE):
        if step > 0:
            for chain in range(CHAINS):
                forward_line(step, chain)
            for chain in range(CHAINS):
                forward_mid(step, chain)
        for chain in range(CHAINS):
            await_core(step, chain)
            product(step, chain)
        for chain in range(CHAINS):
            sigma_after = finish(step, chain, sigma)
        sigma = sigma_after

    group = owned.at[pl.ds(0, count - 1)]
    pltpu.make_async_copy(group, group, tile_send).wait()
    for step in range(DEGREE):
        for chain in range(CHAINS):
            group = low.at[step, chain, pl.ds(0, far - 1)]
            pltpu.make_async_copy(group, group, low_send.at[step, chain]).wait()
            if near > 1:
                group = partial.at[step, chain, pl.ds(0, near - 1)]
                pltpu.make_async_copy(group, group, part_send.at[step, chain]).wait()


def local(start_block, tiles, tile_rows, tile_cols, bounds):
    tall, width = start_block.shape
    tile = tiles.shape[-1]
    slots = tiles.shape[2]
    far = lax.axis_size("row")
    near = lax.axis_size("col")
    assert tall == tile and far % 4 == 0
    count = far * near
    cut = width // CHAINS
    smem = pl.BlockSpec(memory_space=pltpu.SMEM)
    vmem = pl.BlockSpec(memory_space=pltpu.VMEM)
    return pl.pallas_call(
        functools.partial(kernel, far, near, slots, tile, width),
        out_shape=jax.ShapeDtypeStruct((tall, width), jnp.float32),
        in_specs=[smem, smem, smem, vmem, vmem],
        out_specs=vmem,
        scratch_shapes=[
            pltpu.VMEM((slots + 1, tile, tile), jnp.bfloat16),
            pltpu.VMEM((count, tile, tile), jnp.bfloat16),
            pltpu.VMEM((count, tile, tile), jnp.bfloat16),
            pltpu.VMEM((near * tile, far * tile), jnp.bfloat16),
            pltpu.VMEM((tile, tile), jnp.bfloat16),
            pltpu.VMEM((DEGREE, CHAINS, far, tile, cut), jnp.bfloat16),
            pltpu.VMEM((DEGREE, CHAINS, near, tile, cut), jnp.float32),
            pltpu.VMEM((DEGREE, CHAINS, near, tile, cut), jnp.float32),
            pltpu.VMEM((CHAINS, tile, cut), jnp.float32),
            pltpu.VMEM((DEGREE, tile, width), jnp.float32),
            pltpu.SemaphoreType.DMA(()),
            pltpu.SemaphoreType.DMA((far,)),
            pltpu.SemaphoreType.DMA((DEGREE, CHAINS)),
            pltpu.SemaphoreType.DMA((DEGREE, CHAINS, far)),
            pltpu.SemaphoreType.DMA((DEGREE, CHAINS)),
            pltpu.SemaphoreType.DMA((DEGREE, CHAINS, near)),
        ],
        compiler_params=pltpu.CompilerParams(
            collective_id=0, has_side_effects=True, vmem_limit_bytes=60 * 1024 * 1024
        ),
    )(
        tile_rows.reshape(slots),
        tile_cols.reshape(slots),
        bounds,
        start_block,
        tiles.reshape(slots, tile, tile),
    )


def solution(mesh):
    placed = (
        P(("row", "col"), None),
        P("row", "col", None, None, None),
        P("row", "col", None),
        P("row", "col", None),
        P(),
    )
    return jax.shard_map(
        local, mesh=mesh, in_specs=placed, out_specs=P(("row", "col"), None), check_vma=False
    )
```

time: 252 us -> 101 us (0.40)
  waiting for transfers between devices: 195 us -> 0 us
  Pallas kernels: 0 us -> 99 us
  between operations: 17.2 us -> 0.01 us
  starting transfers between devices: 11.5 us -> 0 us
  matrix products: 10.6 us -> 0 us
  other arithmetic: 9.26 us -> 0 us
  local copies, waits for them, and re-layouts: 7.51 us -> 1.57 us
    all_gather x4 -> x0, waiting for transfers between devices: 119 us -> none  [apply_matrix(): lax.all_gather(low_vectors, 'row', axis=0, tiled=True)]
    pallas_call x0 -> x1, Pallas kernels: none -> 99 us  [local(): pl.pallas_call(functools.partial(kernel, far, near, slots, tile, width),...]
    reduce_scatter x4 -> x0, waiting for transfers between devices: 39.2 us -> none  [apply_matrix(): lax.psum_scatter(near_partial.reshape(near_count * tile_size, vec_width),...]
    all_to_all x2 -> x0, waiting for transfers between devices: 37.5 us -> none  [the longest x1 23.3 us: local(): lax.all_to_all(owned, 'row', split_axis=2, concat_axis=2, tiled=True)]
    all_to_all x2 -> x0, starting transfers between devices: 11.1 us -> none  [the longest x1 7.54 us: local(): lax.all_to_all(owned, 'row', split_axis=2, concat_axis=2, tiled=True)]
    dot_general x8 -> x0, matrix products: 10.6 us -> none  [the longest x4 6.63 us: apply_matrix(): jnp.einsum('apxy,pyk->axk', window, far_vectors, preferred_element_type=j...]
    convert_element_type x4 -> x0, other arithmetic: 5.32 us -> none  [apply_matrix(): low_vectors = vectors.astype(jnp.bfloat16)]
    unnamed x20 -> x1, local copies, waits for them, and re-layouts: 4.24 us -> 1.57 us
  transfers between devices with their start and end apart: 10 -> 0, of which waited for: 10 -> 0; matrix products, arithmetic and copies ran while one was open for 1% -> 0% of each run, Pallas kernels for 0% -> 0%
where the time goes in v1:
time: 101 us
  Pallas kernels  99 us (98%)
  local copies, waits for them, and re-layouts  1.57 us (2%)
    pallas_call x1, Pallas kernels, local(): pl.pallas_call(functools.partial(kernel, far, near, slots, tile, width),...  99 us

profile of v1, /device:TPU:0, one launch (start us, length us, event | category | flops | bytes accessed | tf_op | source)
XLA Modules:
  0.0 100.5 jit_solution(8064233061798150297)
XLA Ops:
  0.0 99.0 %shard_map.55 = f32[128,256]{1,0:T(8,128)} custom-call(s32[14]{0:T(128)} %bitcast.4, s32[14]{0:T(128)} %bitcast.5, f32[3]{0:T(128)} %bounds_ref.1, f32[128,256]{1,0:T(8,128)} %start_ref.1, bf16[14,128,128]{2,1,0:T(8,128)(2,1)} %bitcast.3), custom_call_target="tpu_custom_call" | custom-call | tf_op jit(solution)/shard_map/pallas_call | solution.py:255
  99.0 1.6 %copy.7 = f32[128,256]{1,0:T(8,128)} copy(f32[128,256]{1,0:T(8,128)} %shard_map.55) | data formatting | bytes 262144

commit v2 on v1

--- a/solution.py
+++ b/solution.py
@@ -8,7 +8,8 @@
 from jax.sharding import PartitionSpec as P
 
 DEGREE = 4
-CHAINS = 1
+CHAINS = 2
+LAG = 0
 MESH = pl.DeviceIdType.MESH
 
 
@@ -86,6 +87,15 @@
 
     pl.semaphore_wait(barrier, count - 1)
 
+    flip = high >= tall // 2
+    near_end = jnp.where(flip, tall - 1 - high, high)
+
+    def along(position):
+        return jnp.where(flip, tall - 1 - position, position)
+
+    def ranked(index):
+        return index + jnp.where(index >= near_end, 1, 0)
+
     def send_low(step, chain, place, target_row):
         pltpu.make_async_remote_copy(
             src_ref=low.at[step, chain, place],
@@ -101,21 +111,22 @@
         pltpu.make_async_copy(here, here, low_recv.at[step, chain, place]).wait()
 
     def begin(step, chain):
-        for offset in range(1, tall):
-            send_low(step, chain, own_spot, row_of((high + offset) % tall, mid, core))
         send_low(step, chain, own_spot, row_of(high, 1 - mid, core))
+        for index in range(tall - 1):
+            send_low(step, chain, own_spot, row_of(along(ranked(index)), mid, core))
         send_low(step, chain, own_spot, row_of(high, mid, 1 - core))
 
     def forward_line(step, chain):
-        for offset in range(1, tall):
-            place = spot((high + offset) % tall, mid, core)
+        for index in range(tall - 1):
+            place = spot(along(ranked(index)), mid, core)
             await_low(step, chain, place)
             send_low(step, chain, place, row_of(high, 1 - mid, core))
             send_low(step, chain, place, row_of(high, mid, 1 - core))
 
     def forward_mid(step, chain):
-        for offset in range(tall):
-            place = spot((high + offset) % tall, 1 - mid, core)
+        for index in range(tall):
+            source = high if index == 0 else along(ranked(index - 1))
+            place = spot(source, 1 - mid, core)
             await_low(step, chain, place)
             send_low(step, chain, place, row_of(high, mid, 1 - core))
 
@@ -124,17 +135,28 @@
             for mid_at in range(2):
                 await_low(step, chain, spot((high + offset) % tall, mid_at, 1 - core))
 
-    def send_tile(step, carry):
-        other = (me + step) % count
-        pltpu.make_async_remote_copy(
-            src_ref=owned.at[other],
-            dst_ref=mirror.at[me],
-            send_sem=tile_send,
-            recv_sem=tile_recv.at[row],
-            device_id=(other // near, other % near),
-            device_id_type=MESH,
-        ).start()
-        return carry
+    def send_tiles(high_at):
+        inner = me % (4 * near)
+
+        def send_tile(offset, carry):
+            other = high_at * (4 * near) + (inner + offset) % (4 * near)
+            pltpu.make_async_remote_copy(
+                src_ref=owned.at[other],
+                dst_ref=mirror.at[me],
+                send_sem=tile_send,
+                recv_sem=tile_recv.at[row],
+                device_id=(other // near, other % near),
+                device_id_type=MESH,
+            ).start()
+            return carry
+
+        return send_tile
+
+    def send_group(index):
+        if index < 0:
+            lax.fori_loop(1, 4 * near, send_tiles(high), 0)
+        else:
+            lax.fori_loop(0, 4 * near, send_tiles(along(ranked(index))), 0)
 
     def build(step, carry):
         source = (row + far - step) % far
@@ -203,10 +225,11 @@
 
     for chain in range(CHAINS):
         begin(0, chain)
-    lax.fori_loop(1, count // 2, send_tile, 0)
+    groups = list(range(tall - 2, -2, -1))
+    for index in groups:
+        send_group(index)
     for chain in range(CHAINS):
         forward_line(0, chain)
-    lax.fori_loop(count // 2, count, send_tile, 0)
     for chain in range(CHAINS):
         forward_mid(0, chain)
 
@@ -216,19 +239,25 @@
     fill(row)
     lax.fori_loop(1, far, build, 0)
 
-    sigma = sigma_one
-    for step in range(DEGREE):
-        if step > 0:
-            for chain in range(CHAINS):
-                forward_line(step, chain)
-            for chain in range(CHAINS):
-                forward_mid(step, chain)
-        for chain in range(CHAINS):
+    sigmas = [sigma_one] * CHAINS
+
+    def phase(chain, index):
+        step, part = index // 4, index % 4
+        if part == 0:
+            forward_line(step, chain)
+        elif part == 1:
+            forward_mid(step, chain)
+        elif part == 2:
             await_core(step, chain)
             product(step, chain)
+        else:
+            sigmas[chain] = finish(step, chain, sigmas[chain])
+
+    for index in range(2, 4 * DEGREE + LAG * (CHAINS - 1)):
         for chain in range(CHAINS):
-            sigma_after = finish(step, chain, sigma)
-        sigma = sigma_after
+            own_index = index - LAG * chain
+            if 2 <= own_index < 4 * DEGREE:
+                phase(chain, own_index)
 
     group = owned.at[pl.ds(0, count - 1)]
     pltpu.make_async_copy(group, group, tile_send).wait()

time: 101 us -> 87.8 us (0.87)
  Pallas kernels: 99 us -> 86 us
    pallas_call x1, Pallas kernels: 99 us -> 86 us  [local(): pl.pallas_call(functools.partial(kernel, far, near, slots, tile, width),...]
where the time goes in v2:
time: 87.8 us; the launch traced here: 87.6 us
  Pallas kernels  86 us (98%)
  local copies, waits for them, and re-layouts  1.57 us (2%)
    pallas_call x1, Pallas kernels, local(): pl.pallas_call(functools.partial(kernel, far, near, slots, tile, width),...  86 us

profile of v2, /device:TPU:0, one launch (start us, length us, event | category | flops | bytes accessed | tf_op | source)
XLA Modules:
  0.0 87.6 jit_solution(5014590945389934610)
XLA Ops:
  0.0 86.0 %shard_map.55 = f32[128,256]{1,0:T(8,128)} custom-call(s32[14]{0:T(128)} %bitcast.4, s32[14]{0:T(128)} %bitcast.5, f32[3]{0:T(128)} %bounds_ref.1, f32[128,256]{1,0:T(8,128)} %start_ref.1, bf16[14,128,128]{2,1,0:T(8,128)(2,1)} %bitcast.3), custom_call_target="tpu_custom_call" | custom-call | tf_op jit(solution)/shard_map/pallas_call | solution.py:284
  86.1 1.6 %copy.7 = f32[128,256]{1,0:T(8,128)} copy(f32[128,256]{1,0:T(8,128)} %shard_map.55) | data formatting | bytes 262144
